TPU v7x, 32 devices: a whole 2x2x4 slice. The times are simulated.
32 devices in a mesh: seg: 4 (over z), mem: 8 (over y, x, core).
Axes of the slice: x: 2, y: 2, z: 4, core: 2. Of those that a mesh axis runs over, the one named last changes fastest.
Arguments:
- tokens: bfloat16 [8192, 1024], P(('seg', 'mem')), may hold values from -6 to 6
- padding_mask: int32 [8192], P(('seg', 'mem')), may hold values from 0 to 1, as said below
- memory_keys: bfloat16 [4, 8192, 1024], P('seg', 'mem'), may hold values from -6 to 6
- memory_values: bfloat16 [4, 8192, 1024], P('seg', 'mem'), may hold values from -6 to 6
- memory_length: int32 [4], P('seg'), may hold values from 2048 to 8192, as said below
- chosen_keys: int32 [16, 128], P('seg'), may hold values from 0 to 8191, as said below
- norm_gain: float32 [1024], replicated, may hold values from 0.1 to 1.9
- w_query: bfloat16 [1024, 1024], replicated, may hold values from -0.1875 to 0.1875
- w_key: bfloat16 [1024, 1024], replicated, may hold values from -0.1875 to 0.1875
- w_value: bfloat16 [1024, 1024], replicated, may hold values from -0.1875 to 0.1875
- w_out: bfloat16 [1024, 1024], replicated, may hold values from -1.5 to 1.5
- ffn_gain: float32 [1024], replicated, may hold values from 0.1 to 1.9
- w_gate: bfloat16 [1024, 2816], replicated, may hold values from -0.1875 to 0.1875
- w_up: bfloat16 [1024, 2816], replicated, may hold values from -0.1875 to 0.1875
- w_down: bfloat16 [2816, 1024], replicated, may hold values from -0.109375 to 0.109375
- cotangent: bfloat16 [8192, 1024], P(('seg', 'mem')), may hold values from -6 to 6
Outputs:
- mixed: bfloat16 [8192, 1024], P(('seg', 'mem'))
- input_grad: bfloat16 [8192, 1024], P(('seg', 'mem'))
- norm_gain_grad: float32 [1024], P('mem')
- query_grad: float32 [1024, 1024], P('mem')
- key_grad: float32 [1024, 1024], P('mem')
- value_grad: float32 [1024, 1024], P('mem')
- out_grad: float32 [1024, 1024], P('mem')
- ffn_gain_grad: float32 [1024], P('mem')
- gate_grad: float32 [1024, 2816], P('mem')
- up_grad: float32 [1024, 2816], P('mem')
- down_grad: float32 [2816, 1024], P('mem')
Inputs may be any that keep to these rules, and one draw needn't show every extreme that they name: `padding_mask`: within each segment of 2048 consecutive tokens the ones form a prefix of 1024 tokens or more. `memory_length`: how many of a segment's 8192 memory slots are live. `chosen_keys`: row b belongs to the queries b * 512 to (b + 1) * 512 - 1; its first entry is below 2048.
All inputs are finite; a program needn't handle non-finite values.
Results may differ from a plain program's by a relative error of at most 0.014.
Values may be sent and summed in bfloat16 or wider, within the bound.
No kernel may reach another device: no remote copies, remote signals or barrier semaphores. Data moves between devices by JAX's collectives and lax.ppermute only.
A program may use at most 320 MiB of HBM per device.

v0:
```python
import math
import jax
import jax.numpy as jnp
from jax import lax
from jax.sharding import PartitionSpec as P

H = 8
HD = 128
SEG_LEN = 2048
QB = 512
TOPK = 128
EPSILON = 1e-05
NEGATIVE = -1e30


def outer_product(left, right):
    return lax.dot_general(
        left, right, (((0,), (0,)), ((), ())), preferred_element_type=jnp.float32
    )


def backward_dot(left, weight):
    return lax.dot_general(
        left, weight, (((1,), (1,)), ((), ())), preferred_element_type=jnp.float32
    )


def forward_dot(left, weight):
    return jnp.dot(left, weight, preferred_element_type=jnp.float32)


def normalize(values):
    factor = lax.rsqrt(jnp.mean(values * values, axis=-1, keepdims=True) + EPSILON)
    return (values * factor, factor)


def norm_back(grad_in, normed, factor, gain):
    scaled = grad_in * gain
    return factor * (scaled - normed * jnp.mean(scaled * normed, axis=-1, keepdims=True))


def block_stats(scores, usable):
    highest = jnp.max(scores, axis=-1)
    row_sum = jnp.sum(jnp.where(usable, jnp.exp(scores - highest[..., None]), 0.0), axis=-1)
    return (highest, row_sum)


def join_stats(high_left, sum_left, high_right, sum_right):
    highest = jnp.maximum(high_left, high_right)
    return (
        highest,
        sum_left * jnp.exp(high_left - highest) + sum_right * jnp.exp(high_right - highest),
    )


def local(
    tokens,
    padding_mask,
    memory_keys,
    memory_values,
    memory_length,
    chosen_keys,
    norm_gain,
    w_query,
    w_key,
    w_value,
    w_out,
    ffn_gain,
    w_gate,
    w_up,
    w_down,
    cotangent,
):
    group_size = lax.axis_size("mem")
    position = lax.axis_index("mem")
    tok_rows, model_width = tokens.shape
    memory_rows = memory_keys.shape[1]
    segment_count = memory_keys.shape[0]
    all_rows = tok_rows * group_size
    blocks = all_rows // QB
    segment_blocks = SEG_LEN // QB
    score_scale = 1.0 / math.sqrt(HD)
    inputs = tokens.astype(jnp.float32)
    normed_one, factor_one = normalize(inputs)
    h_one = (normed_one * norm_gain).astype(jnp.bfloat16)
    queries = forward_dot(h_one, w_query).astype(jnp.bfloat16)
    keyed_flat = forward_dot(h_one, w_key).astype(jnp.bfloat16)
    valued_flat = forward_dot(h_one, w_value).astype(jnp.bfloat16)
    own_keys = keyed_flat.reshape(tok_rows, H, HD)
    own_values = valued_flat.reshape(tok_rows, H, HD)
    first_row = position * tok_rows
    own_segment = first_row // SEG_LEN
    own_offset = first_row % SEG_LEN
    start_block = own_segment * segment_blocks
    key_position = own_offset + jnp.arange(tok_rows)
    key_usable = padding_mask == 1
    block_segment = jnp.arange(blocks) * QB // SEG_LEN
    segment_match = block_segment[:, None] == jnp.arange(segment_count)[None, :]
    limits = jnp.sum(jnp.where(segment_match, memory_length[None, :], 0), axis=1)
    shifted = chosen_keys - position * memory_rows
    owned = (shifted >= 0) & (shifted < memory_rows) & (chosen_keys < limits[:, None])
    columns = jnp.arange(memory_rows)

    def select_slots(pieces):
        local_rows, usable, segment = pieces
        table = ((local_rows[:, None] == columns[None, :]) & usable[:, None]).astype(jnp.bfloat16)
        keys_here = lax.dynamic_index_in_dim(memory_keys, segment, 0, keepdims=False)
        values_here = lax.dynamic_index_in_dim(memory_values, segment, 0, keepdims=False)
        return (
            forward_dot(table, keys_here).astype(jnp.bfloat16),
            forward_dot(table, values_here).astype(jnp.bfloat16),
        )

    picked_keys, picked_values = lax.map(select_slots, (shifted, owned, block_segment))
    gathered = lax.all_gather(queries, "mem", axis=0, tiled=True).reshape(blocks, QB, H, HD)
    picked_keys = picked_keys.reshape(blocks, TOPK, H, HD)
    picked_values = picked_values.reshape(blocks, TOPK, H, HD)

    def memory_scores(query_block, key_block, usable):
        scores = (
            jnp.einsum("qhd,thd->qht", query_block, key_block, preferred_element_type=jnp.float32)
            * score_scale
        )
        return jnp.where(usable[None, None, :], scores, NEGATIVE)

    def local_visible(block_index):
        query_position = block_index * QB + jnp.arange(QB)
        return (key_position[None, :] <= query_position[:, None]) & key_usable[None, :]

    def local_scores(query_block, visible):
        scores = (
            jnp.einsum("qhd,khd->qhk", query_block, own_keys, preferred_element_type=jnp.float32)
            * score_scale
        )
        return jnp.where(visible[:, None, :], scores, NEGATIVE)

    def segment_rows(source, block_index):
        return lax.dynamic_index_in_dim(source, start_block + block_index, 0, keepdims=False)

    def add_segment(whole, local_part):
        merged = lax.dynamic_slice_in_dim(whole, start_block, segment_blocks, 0) + local_part
        return lax.dynamic_update_slice_in_dim(whole, merged, start_block, 0)

    def memory_first(pieces):
        query_block, key_block, usable = pieces
        return block_stats(memory_scores(query_block, key_block, usable), usable[None, None, :])

    memory_high, memory_sum = lax.map(memory_first, (gathered, picked_keys, owned))

    def local_first(block_index):
        visible = local_visible(block_index)
        scores = local_scores(segment_rows(gathered, block_index), visible)
        return block_stats(scores, visible[:, None, :])

    local_high, local_sum = lax.map(local_first, jnp.arange(segment_blocks))
    seg_high = lax.dynamic_slice_in_dim(memory_high, start_block, segment_blocks, 0)
    seg_sum = lax.dynamic_slice_in_dim(memory_sum, start_block, segment_blocks, 0)
    seg_high, seg_sum = join_stats(seg_high, seg_sum, local_high, local_sum)
    memory_high = lax.dynamic_update_slice_in_dim(memory_high, seg_high, start_block, 0)
    memory_sum = lax.dynamic_update_slice_in_dim(memory_sum, seg_sum, start_block, 0)
    row_high = lax.pmax(memory_high.astype(jnp.bfloat16), "mem").astype(memory_high.dtype)
    row_sum = lax.psum(memory_sum * jnp.exp(memory_high - row_high), "mem")
    log_total = row_high + jnp.log(row_sum)

    def memory_second(pieces):
        query_block, key_block, value_block, usable, block_total = pieces
        scores = memory_scores(query_block, key_block, usable)
        weights = jnp.where(
            usable[None, None, :], jnp.exp(scores - block_total[..., None]), 0.0
        ).astype(jnp.bfloat16)
        return jnp.einsum("qht,thd->qhd", weights, value_block, preferred_element_type=jnp.float32)

    numerators = lax.map(memory_second, (gathered, picked_keys, picked_values, owned, log_total))

    def local_second(block_index):
        visible = local_visible(block_index)
        scores = local_scores(segment_rows(gathered, block_index), visible)
        block_total = segment_rows(log_total, block_index)
        weights = jnp.where(
            visible[:, None, :], jnp.exp(scores - block_total[..., None]), 0.0
        ).astype(jnp.bfloat16)
        return jnp.einsum("qhk,khd->qhd", weights, own_values, preferred_element_type=jnp.float32)

    numerators = add_segment(numerators, lax.map(local_second, jnp.arange(segment_blocks)))
    attended_sum = lax.psum_scatter(
        numerators.reshape(all_rows, model_width), "mem", scatter_dimension=0, tiled=True
    )
    attended = attended_sum.astype(jnp.bfloat16)
    residual = inputs + forward_dot(attended, w_out)
    normed_two, factor_two = normalize(residual)
    h_two = (normed_two * ffn_gain).astype(jnp.bfloat16)
    gate = forward_dot(h_two, w_gate)
    up_part = forward_dot(h_two, w_up)
    sigmoid_gate = jax.nn.sigmoid(gate)
    silu_gate = gate * sigmoid_gate
    act = (silu_gate * up_part).astype(jnp.bfloat16)
    mixed = (residual + forward_dot(act, w_down)).astype(jnp.bfloat16)
    down_grad = outer_product(act, cotangent)
    d_act = backward_dot(cotangent, w_down)
    d_gate = (d_act * up_part * sigmoid_gate * (1.0 + gate * (1.0 - sigmoid_gate))).astype(
        jnp.bfloat16
    )
    d_up = (d_act * silu_gate).astype(jnp.bfloat16)
    gate_grad = outer_product(h_two, d_gate)
    up_grad = outer_product(h_two, d_up)
    d_two = backward_dot(d_gate, w_gate) + backward_dot(d_up, w_up)
    ffn_gain_grad = jnp.sum(d_two * normed_two, axis=0)
    d_res = cotangent.astype(jnp.float32) + norm_back(d_two, normed_two, factor_two, ffn_gain)
    d_res_low = d_res.astype(jnp.bfloat16)
    out_grad = outer_product(attended, d_res_low)
    d_att = backward_dot(d_res_low, w_out).astype(jnp.bfloat16)
    grad_rows = lax.all_gather(d_att, "mem", axis=0, tiled=True).reshape(blocks, QB, H, HD)

    def memory_third(pieces):
        query_block, key_block, value_block, usable, block_total, grad_block = pieces
        scores = memory_scores(query_block, key_block, usable)
        probs = jnp.where(usable[None, None, :], jnp.exp(scores - block_total[..., None]), 0.0)
        pushes = jnp.einsum(
            "qhd,thd->qht", grad_block, value_block, preferred_element_type=jnp.float32
        )
        return jnp.sum(probs * pushes, axis=-1)

    delta_part = lax.map(
        memory_third, (gathered, picked_keys, picked_values, owned, log_total, grad_rows)
    )

    def local_third(block_index):
        visible = local_visible(block_index)
        scores = local_scores(segment_rows(gathered, block_index), visible)
        block_total = segment_rows(log_total, block_index)
        probs = jnp.where(visible[:, None, :], jnp.exp(scores - block_total[..., None]), 0.0)
        pushes = jnp.einsum(
            "qhd,khd->qhk",
            segment_rows(grad_rows, block_index),
            own_values,
            preferred_element_type=jnp.float32,
        )
        return jnp.sum(probs * pushes, axis=-1)

    delta_part = add_segment(delta_part, lax.map(local_third, jnp.arange(segment_blocks)))
    delta = lax.psum(delta_part, "mem")

    def memory_fourth(pieces):
        query_block, key_block, value_block, usable, block_total, grad_block, block_delta = pieces
        scores = memory_scores(query_block, key_block, usable)
        probs = jnp.where(usable[None, None, :], jnp.exp(scores - block_total[..., None]), 0.0)
        pushes = jnp.einsum(
            "qhd,thd->qht", grad_block, value_block, preferred_element_type=jnp.float32
        )
        d_scores = jnp.where(
            usable[None, None, :], probs * (pushes - block_delta[..., None]), 0.0
        ).astype(jnp.bfloat16)
        return (
            jnp.einsum("qht,thd->qhd", d_scores, key_block, preferred_element_type=jnp.float32)
            * score_scale
        )

    query_terms = lax.map(
        memory_fourth, (gathered, picked_keys, picked_values, owned, log_total, grad_rows, delta)
    )

    def local_fourth(running, block_index):
        key_acc, value_acc = running
        visible = local_visible(block_index)
        query_block = segment_rows(gathered, block_index)
        grad_block = segment_rows(grad_rows, block_index)
        scores = local_scores(query_block, visible)
        block_total = segment_rows(log_total, block_index)
        block_delta = segment_rows(delta, block_index)
        probs = jnp.where(visible[:, None, :], jnp.exp(scores - block_total[..., None]), 0.0)
        pushes = jnp.einsum(
            "qhd,khd->qhk", grad_block, own_values, preferred_element_type=jnp.float32
        )
        d_scores = jnp.where(
            visible[:, None, :], probs * (pushes - block_delta[..., None]), 0.0
        ).astype(jnp.bfloat16)
        query_term = (
            jnp.einsum("qhk,khd->qhd", d_scores, own_keys, preferred_element_type=jnp.float32)
            * score_scale
        )
        key_acc = (
            key_acc
            + jnp.einsum("qhk,qhd->khd", d_scores, query_block, preferred_element_type=jnp.float32)
            * score_scale
        )
        value_acc = value_acc + jnp.einsum(
            "qhk,qhd->khd",
            probs.astype(jnp.bfloat16),
            grad_block,
            preferred_element_type=jnp.float32,
        )
        return ((key_acc, value_acc), query_term)

    empty_acc = jnp.zeros((tok_rows, H, HD), jnp.float32)
    (key_sum, value_sum), local_terms = lax.scan(
        local_fourth, (empty_acc, empty_acc), jnp.arange(segment_blocks)
    )
    query_terms = add_segment(query_terms, local_terms)
    d_query = lax.psum_scatter(
        query_terms.reshape(all_rows, model_width), "mem", scatter_dimension=0, tiled=True
    ).astype(jnp.bfloat16)
    d_key = key_sum.reshape(tok_rows, model_width).astype(jnp.bfloat16)
    d_value = value_sum.reshape(tok_rows, model_width).astype(jnp.bfloat16)
    query_grad = outer_product(h_one, d_query)
    key_grad = outer_product(h_one, d_key)
    value_grad = outer_product(h_one, d_value)
    d_one = (
        backward_dot(d_query, w_query) + backward_dot(d_key, w_key) + backward_dot(d_value, w_value)
    )
    norm_gain_grad = jnp.sum(d_one * normed_one, axis=0)
    input_grad = (d_res + norm_back(d_one, normed_one, factor_one, norm_gain)).astype(jnp.bfloat16)
    shards = (
        lax.psum_scatter(norm_gain_grad, "mem", scatter_dimension=0, tiled=True),
        lax.psum_scatter(query_grad, "mem", scatter_dimension=0, tiled=True),
        lax.psum_scatter(key_grad, "mem", scatter_dimension=0, tiled=True),
        lax.psum_scatter(value_grad, "mem", scatter_dimension=0, tiled=True),
        lax.psum_scatter(out_grad, "mem", scatter_dimension=0, tiled=True),
        lax.psum_scatter(ffn_gain_grad, "mem", scatter_dimension=0, tiled=True),
        lax.psum_scatter(gate_grad, "mem", scatter_dimension=0, tiled=True),
        lax.psum_scatter(up_grad, "mem", scatter_dimension=0, tiled=True),
        lax.psum_scatter(down_grad, "mem", scatter_dimension=0, tiled=True),
    )
    (
        norm_part,
        query_part,
        key_part,
        value_part,
        out_part,
        ffn_gain_part,
        gate_part,
        up_grad_part,
        down_part,
    ) = shards
    summed = lax.psum(
        (
            norm_part,
            query_part,
            key_part,
            value_part,
            out_part,
            ffn_gain_part,
            gate_part,
            up_grad_part,
            down_part,
        ),
        "seg",
    )
    (
        norm_done,
        query_done,
        key_done,
        value_done,
        out_done,
        ffn_gain_done,
        gate_done,
        up_done,
        down_done,
    ) = summed
    return (
        mixed,
        input_grad,
        norm_done,
        query_done,
        key_done,
        value_done,
        out_done,
        ffn_gain_done,
        gate_done,
        up_done,
        down_done,
    )


def solution(mesh):
    return jax.shard_map(
        local,
        mesh=mesh,
        in_specs=(
            P(("seg", "mem"), None),
            P(("seg", "mem")),
            P("seg", "mem", None),
            P("seg", "mem", None),
            P("seg"),
            P("seg", None),
            P(),
            P(),
            P(),
            P(),
            P(),
            P(),
            P(),
            P(),
            P(),
            P(("seg", "mem"), None),
        ),
        out_specs=(
            P(("seg", "mem"), None),
            P(("seg", "mem"), None),
            P("mem"),
            P("mem", None),
            P("mem", None),
            P("mem", None),
            P("mem", None),
            P("mem"),
            P("mem", None),
            P("mem", None),
            P("mem", None),
        ),
        check_vma=False,
    )
```

profile of v0, /device:TPU:0, one launch (start us, length us, event | category | flops | bytes accessed | tf_op | source)
XLA Modules:
  0.0 1458.7 jit_solution(2463133091801142676)
XLA Ops:
  15.4 22.5 %while.110 = (s32[]{:T(128)}, bf16[4,128,1024]{2,1,0:T(8,128)(2,1)}, bf16[4,128,1024]{2,1,0:T(8,128)(2,1)}, s32[4,128]{1,0:T(4,128)S(1)}, pred[4,128]{1,0:T(4,12...) while((s32[]{:T(128)}, bf16[4,128,1024]{2,1,0:T(8,128)(2,1)}, ...), condition=%wide.region_2.3_spmd.clone, body=%wide.region_1.2_spmd.clone.sunk | while | flops 537657344 | bytes 4721261 | solution.py:114
  40.4 11.2 all-gather.3.cloned.1.call-done
  57.8 20.9 %while.111 = (s32[]{:T(128)}, f32[4,512,8]{1,2,0:T(8,128)S(1)}, f32[4,512,8]{1,2,0:T(8,128)S(1)}, s32[4]{0:T(128)S(1)}, pred[256]{0:T(512)(128)(4,1)S(1)}, /*ind...) while((s32[]{:T(128)}, f32[4,512,8]{1,2,0:T(8,128)S(1)}, ...), condition=%wide.region_10.11_spmd.clone, body=%wide.region_7.10_spmd.clone.sunk | while | flops 277078784 | bytes 10475995 | solution.py:155
  78.8 9.8 while.106
  88.6 23.5 %pmax.7 = bf16[4,512,8]{1,2,0:T(8,128)(2,1)S(1)} all-reduce(bf16[4,512,8]{1,2,0:T(8,128)(2,1)S(1)} %get-tuple-element.1010), channel_id=1, replica_groups=mesh['seg'=4,'mem'=8] {'mem'}, use_global_device_ids=true, to_apply=%region_11.12 | all-reduce | flops 16384 | bytes 65536 | tf_op jit(solution)/shard_map/pmax | solution.py:161
  119.1 46.3 %all-reduce.9.cloned.1.call-done = f32[4,512,8]{1,2,0:T(8,128)} async-done(((f32[4,512,8]{1,2,0:T(8,128)}), f32[4,512,8]{1,2,0:T(8,128)}) %all-reduce.9.cloned.1.call-update) | async-done | bytes 65552 | tf_op jit(solution)/shard_map/psum | solution.py:162
  166.3 4.2 broadcast.311.clone3.1
  170.5 26.2 %while.112 = (s32[]{:T(128)}, f32[4,512,8,128]{3,1,2,0:T(8,128)}, s32[4]{0:T(128)S(1)}, pred[256]{0:T(512)(128)(4,1)S(1)}, s32[]{:T(128)}, /*index=5*/bf16[4,512...) while((s32[]{:T(128)}, f32[4,512,8,128]{3,1,2,0:T(8,128)}, ...), condition=%wide.region_16.17_spmd.clone, body=%wide.region_15.16_spmd.clone.sunk | while | flops 542376704 | bytes 4643303 | solution.py:184
  172.6 4.4 bitcast_dynamic-update-slice_fusion.17
  179.2 4.4 bitcast_dynamic-update-slice_fusion.17
  185.7 4.5 bitcast_dynamic-update-slice_fusion.17
  192.3 4.5 bitcast_dynamic-update-slice_fusion.17
  201.0 46.6 %while.107 = (s32[]{:T(128)}, f32[4,512,8,128]{3,1,2,0:T(8,128)}, bf16[4,128,8,128]{3,2,1,0:T(8,128)(2,1)}, pred[4,128]{1,0:T(4,128)(4,1)S(1)}, bf16[4,128,8,128...) while((s32[]{:T(128)}, f32[4,512,8,128]{3,1,2,0:T(8,128)}, ...), condition=%wide.region_14.15_spmd, body=%wide.region_13.14_spmd.sunk | while | flops 271056896 | bytes 13158765 | solution.py:173
  247.5 10.3 add.250
  257.8 8.2 copy.98
  266.1 5.3 copy.150
  271.5 70.8 %reduce-scatter.10.cloned.1.call-done = f32[256,1024]{1,0:T(8,128)} async-done(((f32[2048,1024]{1,0:T(8,128)}), f32[256,1024]{1,0:T(8,128)}) %reduce-scatter.10.cloned.1.call-update) | async-done | bytes 1048592 | tf_op jit(solution)/shard_map/reduce_scatter | solution.py:185
  345.4 6.3 fusion.216
  355.0 5.9 multiply_convert_fusion
  370.4 34.3 %all-gather.5.cloned.1.call-done = bf16[2048,1024]{1,0:T(8,128)(2,1)} async-done(((bf16[256,1024]{1,0:T(8,128)(2,1)}), bf16[2048,1024]{1,0:T(8,128)(2,1)}) %all-gather.5.cloned.1.call-update) | async-done | bytes 4194320 | tf_op jit(solution)/shard_map/all_gather | solution.py:212
  410.9 28.1 %while.113 = (s32[]{:T(128)}, f32[4,512,8]{1,2,0:T(8,128)S(1)}, s32[4]{0:T(128)S(1)}, pred[256]{0:T(512)(128)(4,1)S(1)}, s32[]{:T(128)}, /*index=5*/bf16[4,512,8...) while((s32[]{:T(128)}, f32[4,512,8]{1,2,0:T(8,128)S(1)}, ...), condition=%wide.region_25.26_spmd.clone, body=%wide.region_23.25_spmd.clone.sunk | while | flops 543421184 | bytes 12032499 | solution.py:240
  439.0 15.7 %while.108 = (s32[]{:T(128)}, f32[4,512,8]{1,2,0:T(8,128)S(1)}, pred[4,128]{1,0:T(4,128)(4,1)S(1)}, bf16[4,128,8,128]{3,1,2,0:T(8,128)(2,1)}, bf16[4,512,8,128]{...) while((s32[]{:T(128)}, f32[4,512,8]{1,2,0:T(8,128)S(1)}, ...), condition=%wide.region_22.23_spmd, body=%wide.region_20.22_spmd.sunk | while | flops 271577088 | bytes 6917489 | solution.py:223
  455.5 52.6 %all-reduce.11.cloned.1.call-done = f32[4,512,8]{1,2,0:T(8,128)} async-done(((f32[4,512,8]{1,2,0:T(8,128)}), f32[4,512,8]{1,2,0:T(8,128)}) %all-reduce.11.cloned.1.call-update) | async-done | bytes 65552 | tf_op jit(solution)/shard_map/psum | solution.py:241
  512.3 55.4 %while.109 = (s32[]{:T(128)}, f32[4,512,8,128]{3,1,2,0:T(8,128)}, bf16[4,128,8,128]{3,1,2,0:T(8,128)(2,1)}, pred[4,128]{1,0:T(4,128)(4,1)S(1)}, bf16[4,512,8,128...) while((s32[]{:T(128)}, f32[4,512,8,128]{3,1,2,0:T(8,128)}, ...), condition=%wide.region_28.29_spmd, body=%wide.region_27.28_spmd.sunk | while | flops 407371776 | bytes 17665912 | solution.py:258
  515.6 4.6 multiply_bitcast_fusion.2
  529.4 4.6 multiply_bitcast_fusion.2
  543.3 4.6 multiply_bitcast_fusion.2
  557.0 4.6 multiply_bitcast_fusion.2
  571.9 50.7 %while.114 = (s32[]{:T(128)}, f32[256,8,128]{0,2,1:T(8,128)}, f32[256,8,128]{0,2,1:T(8,128)}, f32[4,512,8,128]{3,1,2,0:T(8,128)}, s32[4]{0:T(128)S(1)}, /*index=...) while((s32[]{:T(128)}, f32[256,8,128]{0,2,1:T(8,128)}, ...), condition=%wide.region_30.31_spmd.clone, body=%wide.region_29.30_spmd.clone.sunk | while | flops 1357906688 | bytes 65264296 | solution.py:295
  622.6 10.3 add.259
  632.9 8.2 copy.117
  641.1 5.4 copy.149
  646.6 4.4 fusion.199
  661.5 7.7 fusion.219
  669.2 7.4 fusion.218
  676.7 7.6 fusion.220
  684.4 33.0 %reduce-scatter.12.cloned.1.call-done = f32[256,1024]{1,0:T(8,128)} async-done(((f32[2048,1024]{1,0:T(8,128)}), f32[256,1024]{1,0:T(8,128)}) %reduce-scatter.12.cloned.1.call-update) | async-done | bytes 1048592 | tf_op jit(solution)/shard_map/reduce_scatter | solution.py:299
  721.5 50.6 %reduce-scatter.20.cloned.1.call-done = f32[128,1024]{1,0:T(8,128)} async-done(((f32[1024,1024]{1,0:T(8,128)}), f32[128,1024]{1,0:T(8,128)}) %reduce-scatter.20.cloned.1.call-update) | async-done | bytes 524304 | tf_op jit(solution)/shard_map/reduce_scatter | solution.py:317
  772.1 55.1 %reduce-scatter.18.cloned.1.call-done = f32[128,1024]{1,0:T(8,128)} async-done(((f32[1024,1024]{1,0:T(8,128)}), f32[128,1024]{1,0:T(8,128)}) %reduce-scatter.18.cloned.1.call-update) | async-done | bytes 524304 | tf_op jit(solution)/shard_map/reduce_scatter | solution.py:316
  827.2 54.7 %reduce-scatter.16.cloned.1.call-done = f32[128,1024]{1,0:T(8,128)} async-done(((f32[1024,1024]{1,0:T(8,128)}), f32[128,1024]{1,0:T(8,128)}) %reduce-scatter.16.cloned.1.call-update) | async-done | bytes 524304 | tf_op jit(solution)/shard_map/reduce_scatter | solution.py:315
  881.9 90.6 %reduce-scatter.24.cloned.1.call-done = f32[128,2816]{1,0:T(8,128)} async-done(((f32[1024,2816]{1,0:T(8,128)}), f32[128,2816]{1,0:T(8,128)}) %reduce-scatter.24.cloned.1.call-update) | async-done | bytes 1441808 | tf_op jit(solution)/shard_map/reduce_scatter | solution.py:320
  972.4 90.7 %reduce-scatter.22.cloned.1.call-done = f32[128,2816]{1,0:T(8,128)} async-done(((f32[1024,2816]{1,0:T(8,128)}), f32[128,2816]{1,0:T(8,128)}) %reduce-scatter.22.cloned.1.call-update) | async-done | bytes 1441808 | tf_op jit(solution)/shard_map/reduce_scatter | solution.py:319
  1063.1 90.5 %reduce-scatter.26.cloned.1.call-done = f32[352,1024]{1,0:T(8,128)} async-done(((f32[2816,1024]{1,0:T(8,128)}), f32[352,1024]{1,0:T(8,128)}) %reduce-scatter.26.cloned.1.call-update) | async-done | bytes 1441808 | tf_op jit(solution)/shard_map/reduce_scatter | solution.py:321
  1153.7 55.0 %reduce-scatter.14.cloned.1.call-done = f32[128,1024]{1,0:T(8,128)} async-done(((f32[1024,1024]{1,0:T(8,128)}), f32[128,1024]{1,0:T(8,128)}) %reduce-scatter.14.cloned.1.call-update) | async-done | bytes 524304 | tf_op jit(solution)/shard_map/reduce_scatter | solution.py:314
  1210.0 5.9 fusion.184
  1221.0 13.1 all-reduce.2
  1234.3 12.5 all-reduce.3
  1249.5 191.5 %all-reduce.13.cloned.1.call-done = (f32[128,1024]{1,0:T(8,128)}, f32[128,1024]{1,0:T(8,128)}, f32[128,1024]{1,0:T(8,128)}, f32[128,1024]{1,0:T(8,128)}, f32[128...) async-done(((f32[128,1024]{1,0:T(8,128)}, f32[128,1024]{1,0:T(8,128)}, f32[128,1024]{1,0:T(8,128)}, f32[128,1024]{1,0:T(8,128)}, f32[128,2816]{1,0:T(8,128)}, ...) | async-done | bytes 6422544 | tf_op jit(solution)/shard_map/psum | solution.py:334
  (429 shorter events, 309.7 us)
Async XLA Ops:
  7.2 106.0 %copy-start = (bf16[1024,1024]{1,0:T(8,128)(2,1)S(1)}, bf16[1024,1024]{1,0:T(8,128)(2,1)}, u32[]{:S(2)}) copy-start(bf16[1024,1024]{1,0:T(8,128)(2,1)} %param.43) | copy-start | bytes 6291460
  7.2 5.6 copy-start.3
  7.2 5.6 copy-start.25
  7.2 44.4 %all-gather.3.cloned.1.call-start = ((), (), s32[]{:S(2)}) async-start(), calls=%async_computation.9 | async-start | bytes 4718592 | tf_op jit(solution)/shard_map/all_gather | solution.py:115
  8.6 104.5 %copy-start.27 = (f32[256]{0:T(256)}, f32[256]{0:T(256)S(1)}, u32[]{:S(2)}) copy-start(f32[256]{0:T(256)S(1)} %add_rsqrt_fusion.1) | copy-start | bytes 3076
  8.7 6.6 copy-start.32
  8.7 6.7 copy-start.30
  12.1 153.4 %all-reduce.9.cloned.1.call-start = ((), (), s32[]{:S(2)}) async-start(), calls=%async_computation.10 | async-start | bytes 131072 | tf_op jit(solution)/shard_map/psum | solution.py:162
  112.8 229.5 %reduce-scatter.10.cloned.1.call-start = ((), (), s32[]{:S(2)}) async-start(), calls=%async_computation.11 | async-start | bytes 9437184 | tf_op jit(solution)/shard_map/reduce_scatter | solution.py:185
  271.5 73.7 %copy-start.29 = (f32[1024]{0:T(1024)S(1)}, f32[1024]{0:T(1024)}, u32[]{:S(2)}) copy-start(f32[1024]{0:T(1024)} %param.45) | copy-start | bytes 12292
  271.5 133.3 %all-gather.5.cloned.1.call-start = ((), (), s32[]{:S(2)}) async-start(), calls=%async_computation.12 | async-start | bytes 4718592 | tf_op jit(solution)/shard_map/all_gather | solution.py:212
  342.3 9.4 slice-start
  345.1 19.9 %copy-start.6 = (f32[256,1024]{1,0:T(8,128)}, f32[256,1024]{1,0:T(8,128)S(1)}, u32[]{:S(2)}) copy-start(f32[256,1024]{1,0:T(8,128)S(1)} %get-tuple-element.1028) | copy-start | bytes 3145732
  345.3 6.3 copy-start.10
  345.3 6.3 slice-start.1
  345.4 9.6 slice-start.4
  351.7 3.3 copy-start.15
  351.7 3.3 slice-start.5
  351.7 10.9 slice-start.2
  355.0 7.6 slice-start.3
  362.6 3.7 copy-start.7
  367.9 140.2 %all-reduce.11.cloned.1.call-start = ((), (), s32[]{:S(2)}) async-start(), calls=%async_computation.13 | async-start | bytes 131072 | tf_op jit(solution)/shard_map/psum | solution.py:241
  408.0 2.9 copy-start.23
  455.4 261.9 %reduce-scatter.12.cloned.1.call-start = ((), (), s32[]{:S(2)}) async-start(), calls=%async_computation.14 | async-start | bytes 9437184 | tf_op jit(solution)/shard_map/reduce_scatter | solution.py:299
  508.0 4.2 copy-start.24
  573.8 2.5 copy-start.11
  573.8 2.8 copy-start.21
  586.3 2.5 copy-start.11
  586.4 2.8 copy-start.21
  598.9 2.5 copy-start.11
  598.9 2.8 copy-start.21
  611.5 2.5 copy-start.11
  611.5 2.8 copy-start.21
  646.5 125.5 %reduce-scatter.20.cloned.1.call-start = ((), (), s32[]{:S(2)}) async-start(), calls=%async_computation.18 | async-start | bytes 4718592 | tf_op jit(solution)/shard_map/reduce_scatter | solution.py:317
  651.0 176.2 %reduce-scatter.18.cloned.1.call-start = ((), (), s32[]{:S(2)}) async-start(), calls=%async_computation.17 | async-start | bytes 4718592 | tf_op jit(solution)/shard_map/reduce_scatter | solution.py:316
  655.9 226.0 %reduce-scatter.16.cloned.1.call-start = ((), (), s32[]{:S(2)}) async-start(), calls=%async_computation.16 | async-start | bytes 4718592 | tf_op jit(solution)/shard_map/reduce_scatter | solution.py:315
  661.2 311.2 %reduce-scatter.24.cloned.1.call-start = ((), (), s32[]{:S(2)}) async-start(), calls=%async_computation.20 | async-start | bytes 12976128 | tf_op jit(solution)/shard_map/reduce_scatter | solution.py:320
  669.1 394.0 %reduce-scatter.22.cloned.1.call-start = ((), (), s32[]{:S(2)}) async-start(), calls=%async_computation.19 | async-start | bytes 12976128 | tf_op jit(solution)/shard_map/reduce_scatter | solution.py:319
  676.7 477.0 %reduce-scatter.26.cloned.1.call-start = ((), (), s32[]{:S(2)}) async-start(), calls=%async_computation.21 | async-start | bytes 12976128 | tf_op jit(solution)/shard_map/reduce_scatter | solution.py:321
  684.3 524.4 %reduce-scatter.14.cloned.1.call-start = ((), (), s32[]{:S(2)}) async-start(), calls=%async_computation.15 | async-start | bytes 4718592 | tf_op jit(solution)/shard_map/reduce_scatter | solution.py:314
  721.4 487.3 %copy-start.33 = (u32[32]{0:T(128)S(1)}, u32[32]{0:T(128)}, u32[]{:S(2)}) copy-start(u32[32]{0:T(128)} %constant.261) | copy-start | bytes 388
  721.4 719.5 %all-reduce.13.cloned.1.call-start = ((), (), s32[]{:S(2)}) async-start(), calls=%async_computation.22 | async-start | bytes 12845056 | tf_op jit(solution)/shard_map/psum | solution.py:334
  1210.0 5.9 copy-start.12
  1210.0 5.9 copy-start.13
  1218.4 2.7 copy-start.31
  1440.9 7.8 copy-start.20
  1440.9 8.9 copy-start.19
  1443.0 8.0 copy-start.18
  (21 other events, 39.3 us)
Sparse Core Ops, SparseCore 0:
  12.2 39.4 all-gather.2
  112.9 52.4 all-reduce.8
  271.6 70.6 reduce-scatter.9
  368.0 36.7 all-gather.4
  455.5 52.4 all-reduce.10
  646.7 70.6 reduce-scatter.11
  720.7 51.3 reduce-scatter.19
  775.8 51.3 reduce-scatter.17
  830.5 51.2 reduce-scatter.15
  885.6 86.7 reduce-scatter.23
  976.3 86.7 reduce-scatter.21
  1066.9 86.7 reduce-scatter.25
  1157.4 51.2 reduce-scatter.13
  1211.5 229.3 all-reduce.12
where the time goes:
time: 1470 us; the launch traced here: 1460 us
  waiting for transfers between devices  927 us (63%)
  matrix products  254 us (17%)
  local copies, waits for them, and re-layouts  149 us (10%)
  blocking collectives  49.1 us (3%)
  other arithmetic  39.6 us (3%)
  loops' own time  23.4 us (2%)
  between operations  16.1 us (1%)
    psum x1, waiting for transfers between devices, local(): lax.psum((norm_part, query_part, key_part, value_part, out_part, ffn_gain...  191 us
    reduce_scatter x1, waiting for transfers between devices, local(): lax.psum_scatter(gate_grad, 'mem', scatter_dimension=0, tiled=True)  90.7 us
    reduce_scatter x1, waiting for transfers between devices, local(): lax.psum_scatter(up_grad, 'mem', scatter_dimension=0, tiled=True)  90.6 us
    reduce_scatter x1, waiting for transfers between devices, local(): lax.psum_scatter(down_grad, 'mem', scatter_dimension=0, tiled=True)  90.5 us
    reduce_scatter x1, waiting for transfers between devices, local(): lax.psum_scatter(numerators.reshape(all_rows, model_width), 'mem', scatte...  70.8 us
    reduce_scatter x1, waiting for transfers between devices, local(): lax.psum_scatter(value_grad, 'mem', scatter_dimension=0, tiled=True)  55.1 us
    reduce_scatter x1, waiting for transfers between devices, local(): lax.psum_scatter(query_grad, 'mem', scatter_dimension=0, tiled=True)  55 us
    reduce_scatter x1, waiting for transfers between devices, local(): lax.psum_scatter(key_grad, 'mem', scatter_dimension=0, tiled=True)  54.7 us
  transfers between devices with their start and end apart: 14, of which 14 were waited for; matrix products, arithmetic and copies ran while one was open for 6% of the time, Pallas kernels for 0%

commit v1 on v0

--- a/solution.py
+++ b/solution.py
@@ -3,6 +3,7 @@
 import jax.numpy as jnp
 from jax import lax
 from jax.sharding import PartitionSpec as P
+from jax.lax import all_to_all, axis_size
 
 H = 8
 HD = 128
@@ -11,6 +12,13 @@
 TOPK = 128
 EPSILON = 1e-05
 NEGATIVE = -1e30
+
+
+def see_yards(work_x):
+    fields = []
+    for _ in range(axis_size("mem")):
+        fields.append(work_x)
+    return jnp.concatenate(all_to_all(jnp.stack(fields, axis=0), "mem", 0, 0), axis=0)
 
 
 def outer_product(left, right):
@@ -209,7 +217,7 @@
     d_res_low = d_res.astype(jnp.bfloat16)
     out_grad = outer_product(attended, d_res_low)
     d_att = backward_dot(d_res_low, w_out).astype(jnp.bfloat16)
-    grad_rows = lax.all_gather(d_att, "mem", axis=0, tiled=True).reshape(blocks, QB, H, HD)
+    grad_rows = see_yards(d_att).reshape(blocks, QB, H, HD)
 
     def memory_third(pieces):
         query_block, key_block, value_block, usable, block_total, grad_block = pieces

time: 1470 us -> 1490 us (1.014)
    all_to_all x0 -> x1, waiting for transfers between devices: none -> 46.6 us  [see_yards(): all_to_all(jnp.stack(fields, axis=0), 'mem', 0, 0)]
    all_gather x1 -> x0, waiting for transfers between devices: 34.3 us -> none  [local(): lax.all_gather(d_att, 'mem', axis=0, tiled=True).reshape(blocks, QB, H, HD)]
    unnamed x85 -> x99, local copies, waits for them, and re-layouts: 35.1 us -> 39.1 us
where the time goes in v1:
time: 1490 us; the launch traced here: 1480 us
  waiting for transfers between devices  936 us (63%)
  matrix products  254 us (17%)
  local copies, waits for them, and re-layouts  155 us (10%)
  blocking collectives  49.2 us (3%)
  other arithmetic  36.7 us (2%)
  loops' own time  23.4 us (2%)
  between operations  16.1 us (1%)
    psum x1, waiting for transfers between devices, local(): lax.psum((norm_part, query_part, key_part, value_part, out_part, ffn_gain...  192 us
    reduce_scatter x1, waiting for transfers between devices, local(): lax.psum_scatter(up_grad, 'mem', scatter_dimension=0, tiled=True)  90.7 us
    reduce_scatter x1, waiting for transfers between devices, local(): lax.psum_scatter(down_grad, 'mem', scatter_dimension=0, tiled=True)  90.7 us
    reduce_scatter x1, waiting for transfers between devices, local(): lax.psum_scatter(gate_grad, 'mem', scatter_dimension=0, tiled=True)  90.5 us
    reduce_scatter x1, waiting for transfers between devices, local(): lax.psum_scatter(numerators.reshape(all_rows, model_width), 'mem', scatte...  70.8 us
    reduce_scatter x1, waiting for transfers between devices, local(): lax.psum_scatter(value_grad, 'mem', scatter_dimension=0, tiled=True)  55.1 us
    reduce_scatter x1, waiting for transfers between devices, local(): lax.psum_scatter(query_grad, 'mem', scatter_dimension=0, tiled=True)  54.9 us
    reduce_scatter x1, waiting for transfers between devices, local(): lax.psum_scatter(key_grad, 'mem', scatter_dimension=0, tiled=True)  54.7 us
  transfers between devices with their start and end apart: 14, of which 14 were waited for; matrix products, arithmetic and copies ran while one was open for 6% of the time, Pallas kernels for 0%

profile of v1, /device:TPU:0, one launch (start us, length us, event | category | flops | bytes accessed | tf_op | source)
XLA Modules:
  0.0 1477.1 jit_solution(15884620019467557923)
XLA Ops:
  15.4 22.5 %while.110 = (s32[]{:T(128)}, bf16[4,128,1024]{2,1,0:T(8,128)(2,1)}, bf16[4,128,1024]{2,1,0:T(8,128)(2,1)}, s32[4,128]{1,0:T(4,128)S(1)}, pred[4,128]{1,0:T(4,12...) while((s32[]{:T(128)}, bf16[4,128,1024]{2,1,0:T(8,128)(2,1)}, ...), condition=%wide.region_2.3_spmd.clone, body=%wide.region_1.2_spmd.clone.sunk | while | flops 537657344 | bytes 4721261 | solution.py:122
  40.4 11.4 all-gather.2.cloned.1.call-done
  58.0 20.9 %while.111 = (s32[]{:T(128)}, f32[4,512,8]{1,2,0:T(8,128)S(1)}, f32[4,512,8]{1,2,0:T(8,128)S(1)}, s32[4]{0:T(128)S(1)}, pred[256]{0:T(512)(128)(4,1)S(1)}, /*ind...) while((s32[]{:T(128)}, f32[4,512,8]{1,2,0:T(8,128)S(1)}, ...), condition=%wide.region_10.11_spmd.clone, body=%wide.region_7.10_spmd.clone.sunk | while | flops 277078784 | bytes 10475995 | solution.py:163
  78.9 9.8 while.106
  88.7 23.5 %pmax.7 = bf16[4,512,8]{1,2,0:T(8,128)(2,1)S(1)} all-reduce(bf16[4,512,8]{1,2,0:T(8,128)(2,1)S(1)} %get-tuple-element.1010), channel_id=1, replica_groups=mesh['seg'=4,'mem'=8] {'mem'}, use_global_device_ids=true, to_apply=%region_11.12 | all-reduce | flops 16384 | bytes 65536 | tf_op jit(solution)/shard_map/pmax | solution.py:169
  119.3 46.3 %all-reduce.9.cloned.1.call-done = f32[4,512,8]{1,2,0:T(8,128)} async-done(((f32[4,512,8]{1,2,0:T(8,128)}), f32[4,512,8]{1,2,0:T(8,128)}) %all-reduce.9.cloned.1.call-update) | async-done | bytes 65552 | tf_op jit(solution)/shard_map/psum | solution.py:170
  170.7 26.3 %while.112 = (s32[]{:T(128)}, f32[4,512,8,128]{3,1,2,0:T(8,128)}, s32[4]{0:T(128)S(1)}, pred[256]{0:T(512)(128)(4,1)S(1)}, s32[]{:T(128)}, /*index=5*/bf16[4,512...) while((s32[]{:T(128)}, f32[4,512,8,128]{3,1,2,0:T(8,128)}, ...), condition=%wide.region_16.17_spmd.clone, body=%wide.region_15.16_spmd.clone.sunk | while | flops 542376704 | bytes 4643303 | solution.py:192
  172.8 4.5 bitcast_dynamic-update-slice_fusion.17
  179.3 4.4 bitcast_dynamic-update-slice_fusion.17
  185.9 4.5 bitcast_dynamic-update-slice_fusion.17
  192.4 4.5 bitcast_dynamic-update-slice_fusion.17
  201.2 46.7 %while.107 = (s32[]{:T(128)}, f32[4,512,8,128]{3,1,2,0:T(8,128)}, bf16[4,128,8,128]{3,2,1,0:T(8,128)(2,1)}, pred[4,128]{1,0:T(4,128)(4,1)S(1)}, bf16[4,128,8,128...) while((s32[]{:T(128)}, f32[4,512,8,128]{3,1,2,0:T(8,128)}, ...), condition=%wide.region_14.15_spmd, body=%wide.region_13.14_spmd.sunk | while | flops 271056896 | bytes 13158765 | solution.py:181
  247.9 10.3 add.250
  258.2 8.2 copy.96
  266.4 5.4 copy.148
  271.8 70.8 %reduce-scatter.10.cloned.1.call-done = f32[256,1024]{1,0:T(8,128)} async-done(((f32[2048,1024]{1,0:T(8,128)}), f32[256,1024]{1,0:T(8,128)}) %reduce-scatter.10.cloned.1.call-update) | async-done | bytes 1048592 | tf_op jit(solution)/shard_map/reduce_scatter | solution.py:193
  345.8 6.3 fusion.216
  355.4 5.9 multiply_convert_fusion
  370.0 4.5 all-to-all-start
  377.1 46.6 %all-to-all-done = bf16[8,256,1024]{2,1,0:T(8,128)(2,1)} async-done(((bf16[8,256,1024]{2,1,0:T(8,128)(2,1)}), bf16[8,256,1024]{2,1,0:T(8,128)(2,1)}, u32[]{:S(2)}, u32[]{:S(2)}) %all-to-all-start) | async-done | bytes 4194336 | tf_op jit(solution)/shard_map/all_to_all | solution.py:21
  429.9 28.1 %while.113 = (s32[]{:T(128)}, f32[4,512,8]{1,2,0:T(8,128)S(1)}, s32[4]{0:T(128)S(1)}, pred[256]{0:T(512)(128)(4,1)S(1)}, s32[]{:T(128)}, /*index=5*/bf16[4,512,8...) while((s32[]{:T(128)}, f32[4,512,8]{1,2,0:T(8,128)S(1)}, ...), condition=%wide.region_25.26_spmd.clone, body=%wide.region_23.25_spmd.clone.sunk | while | flops 543421184 | bytes 12032499 | solution.py:248
  458.0 15.7 %while.108 = (s32[]{:T(128)}, f32[4,512,8]{1,2,0:T(8,128)S(1)}, pred[4,128]{1,0:T(4,128)(4,1)S(1)}, bf16[4,128,8,128]{3,1,2,0:T(8,128)(2,1)}, bf16[4,512,8,128]{...) while((s32[]{:T(128)}, f32[4,512,8]{1,2,0:T(8,128)S(1)}, ...), condition=%wide.region_22.23_spmd, body=%wide.region_20.22_spmd.sunk | while | flops 271577088 | bytes 6917489 | solution.py:231
  474.4 51.7 %all-reduce.11.cloned.1.call-done = f32[4,512,8]{1,2,0:T(8,128)} async-done(((f32[4,512,8]{1,2,0:T(8,128)}), f32[4,512,8]{1,2,0:T(8,128)}) %all-reduce.11.cloned.1.call-update) | async-done | bytes 65552 | tf_op jit(solution)/shard_map/psum | solution.py:249
  530.3 55.5 %while.109 = (s32[]{:T(128)}, f32[4,512,8,128]{3,1,2,0:T(8,128)}, bf16[4,128,8,128]{3,1,2,0:T(8,128)(2,1)}, pred[4,128]{1,0:T(4,128)(4,1)S(1)}, bf16[4,512,8,128...) while((s32[]{:T(128)}, f32[4,512,8,128]{3,1,2,0:T(8,128)}, ...), condition=%wide.region_28.29_spmd, body=%wide.region_27.28_spmd.sunk | while | flops 407371776 | bytes 17665912 | solution.py:266
  533.7 4.6 multiply_bitcast_fusion.2
  547.6 4.6 multiply_bitcast_fusion.2
  561.4 4.6 multiply_bitcast_fusion.2
  575.2 4.6 multiply_bitcast_fusion.2
  590.1 50.7 %while.114 = (s32[]{:T(128)}, f32[256,8,128]{0,2,1:T(8,128)}, f32[256,8,128]{0,2,1:T(8,128)}, f32[4,512,8,128]{3,1,2,0:T(8,128)}, s32[4]{0:T(128)S(1)}, /*index=...) while((s32[]{:T(128)}, f32[256,8,128]{0,2,1:T(8,128)}, ...), condition=%wide.region_30.31_spmd.clone, body=%wide.region_29.30_spmd.clone.sunk | while | flops 1357906688 | bytes 65264296 | solution.py:303
  640.8 10.3 add.259
  651.1 8.2 copy.115
  659.4 5.4 copy.147
  672.1 4.3 fusion.206
  681.7 7.4 fusion.219
  689.2 7.5 fusion.218
  697.7 7.5 fusion.220
  705.2 30.4 %reduce-scatter.12.cloned.1.call-done = f32[256,1024]{1,0:T(8,128)} async-done(((f32[2048,1024]{1,0:T(8,128)}), f32[256,1024]{1,0:T(8,128)}) %reduce-scatter.12.cloned.1.call-update) | async-done | bytes 1048592 | tf_op jit(solution)/shard_map/reduce_scatter | solution.py:307
  739.8 50.5 %reduce-scatter.20.cloned.1.call-done = f32[128,1024]{1,0:T(8,128)} async-done(((f32[1024,1024]{1,0:T(8,128)}), f32[128,1024]{1,0:T(8,128)}) %reduce-scatter.20.cloned.1.call-update) | async-done | bytes 524304 | tf_op jit(solution)/shard_map/reduce_scatter | solution.py:325
  790.2 55.1 %reduce-scatter.18.cloned.1.call-done = f32[128,1024]{1,0:T(8,128)} async-done(((f32[1024,1024]{1,0:T(8,128)}), f32[128,1024]{1,0:T(8,128)}) %reduce-scatter.18.cloned.1.call-update) | async-done | bytes 524304 | tf_op jit(solution)/shard_map/reduce_scatter | solution.py:324
  845.3 54.7 %reduce-scatter.16.cloned.1.call-done = f32[128,1024]{1,0:T(8,128)} async-done(((f32[1024,1024]{1,0:T(8,128)}), f32[128,1024]{1,0:T(8,128)}) %reduce-scatter.16.cloned.1.call-update) | async-done | bytes 524304 | tf_op jit(solution)/shard_map/reduce_scatter | solution.py:323
  900.0 90.7 %reduce-scatter.24.cloned.1.call-done = f32[128,2816]{1,0:T(8,128)} async-done(((f32[1024,2816]{1,0:T(8,128)}), f32[128,2816]{1,0:T(8,128)}) %reduce-scatter.24.cloned.1.call-update) | async-done | bytes 1441808 | tf_op jit(solution)/shard_map/reduce_scatter | solution.py:328
  990.7 90.5 %reduce-scatter.22.cloned.1.call-done = f32[128,2816]{1,0:T(8,128)} async-done(((f32[1024,2816]{1,0:T(8,128)}), f32[128,2816]{1,0:T(8,128)}) %reduce-scatter.22.cloned.1.call-update) | async-done | bytes 1441808 | tf_op jit(solution)/shard_map/reduce_scatter | solution.py:327
  1081.2 90.7 %reduce-scatter.26.cloned.1.call-done = f32[352,1024]{1,0:T(8,128)} async-done(((f32[2816,1024]{1,0:T(8,128)}), f32[352,1024]{1,0:T(8,128)}) %reduce-scatter.26.cloned.1.call-update) | async-done | bytes 1441808 | tf_op jit(solution)/shard_map/reduce_scatter | solution.py:329
  1171.9 54.9 %reduce-scatter.14.cloned.1.call-done = f32[128,1024]{1,0:T(8,128)} async-done(((f32[1024,1024]{1,0:T(8,128)}), f32[128,1024]{1,0:T(8,128)}) %reduce-scatter.14.cloned.1.call-update) | async-done | bytes 524304 | tf_op jit(solution)/shard_map/reduce_scatter | solution.py:322
  1228.2 5.9 fusion.184
  1239.2 13.2 all-reduce.2
  1252.5 12.5 all-reduce.3
  1267.7 191.5 %all-reduce.13.cloned.1.call-done = (f32[128,1024]{1,0:T(8,128)}, f32[128,1024]{1,0:T(8,128)}, f32[128,1024]{1,0:T(8,128)}, f32[128,1024]{1,0:T(8,128)}, f32[128...) async-done(((f32[128,1024]{1,0:T(8,128)}, f32[128,1024]{1,0:T(8,128)}, f32[128,1024]{1,0:T(8,128)}, f32[128,1024]{1,0:T(8,128)}, f32[128,2816]{1,0:T(8,128)}, ...) | async-done | bytes 6422544 | tf_op jit(solution)/shard_map/psum | solution.py:342
  (443 shorter events, 318.9 us)
Async XLA Ops:
  7.2 106.1 %copy-start = (bf16[1024,1024]{1,0:T(8,128)(2,1)S(1)}, bf16[1024,1024]{1,0:T(8,128)(2,1)}, u32[]{:S(2)}) copy-start(bf16[1024,1024]{1,0:T(8,128)(2,1)} %param.43) | copy-start | bytes 6291460
  7.2 5.6 copy-start.4
  7.2 5.6 copy-start.32
  7.2 44.5 %all-gather.2.cloned.1.call-start = ((), (), s32[]{:S(2)}) async-start(), calls=%async_computation.10 | async-start | bytes 4718592 | tf_op jit(solution)/shard_map/all_gather | solution.py:123
  8.6 104.6 %copy-start.34 = (f32[256]{0:T(256)}, f32[256]{0:T(256)S(1)}, u32[]{:S(2)}) copy-start(f32[256]{0:T(256)S(1)} %add_rsqrt_fusion.1) | copy-start | bytes 3076
  8.7 6.6 copy-start.39
  8.7 6.7 copy-start.37
  12.1 153.5 %all-reduce.9.cloned.1.call-start = ((), (), s32[]{:S(2)}) async-start(), calls=%async_computation.11 | async-start | bytes 131072 | tf_op jit(solution)/shard_map/psum | solution.py:170
  112.9 229.7 %reduce-scatter.10.cloned.1.call-start = ((), (), s32[]{:S(2)}) async-start(), calls=%async_computation.12 | async-start | bytes 9437184 | tf_op jit(solution)/shard_map/reduce_scatter | solution.py:193
  271.8 73.7 %copy-start.36 = (f32[1024]{0:T(1024)S(1)}, f32[1024]{0:T(1024)}, u32[]{:S(2)}) copy-start(f32[1024]{0:T(1024)} %param.45) | copy-start | bytes 12292
  342.7 9.4 slice-start
  345.5 19.8 %copy-start.8 = (f32[256,1024]{1,0:T(8,128)}, f32[256,1024]{1,0:T(8,128)S(1)}, u32[]{:S(2)}) copy-start(f32[256,1024]{1,0:T(8,128)S(1)} %get-tuple-element.1028) | copy-start | bytes 3145732
  345.7 6.3 copy-start.14
  345.7 6.3 slice-start.1
  345.8 9.6 slice-start.4
  352.1 3.3 copy-start.20
  352.1 3.3 slice-start.5
  352.1 10.8 slice-start.2
  355.3 7.6 slice-start.3
  363.0 3.7 copy-start.9
  370.0 53.7 %all-to-all-start = ((bf16[8,256,1024]{2,1,0:T(8,128)(2,1)}), bf16[8,256,1024]{2,1,0:T(8,128)(2,1)}, u32[]{:S(2)}, u32[]{:S(2)}) async-start(bf16[8,256,1024]{2,1,0:T(8,128)(2,1)} %stack.2), calls=%async_computation.1 | async-start | bytes 8388608 | tf_op jit(solution)/shard_map/all_to_all | solution.py:21
  374.5 151.6 %all-reduce.11.cloned.1.call-start = ((), (), s32[]{:S(2)}) async-start(), calls=%async_computation.13 | async-start | bytes 131072 | tf_op jit(solution)/shard_map/psum | solution.py:249
  427.0 2.9 copy-start.30
  474.4 261.3 %reduce-scatter.12.cloned.1.call-start = ((), (), s32[]{:S(2)}) async-start(), calls=%async_computation.14 | async-start | bytes 9437184 | tf_op jit(solution)/shard_map/reduce_scatter | solution.py:307
  526.1 4.2 copy-start.31
  592.0 2.8 copy-start.27
  604.5 2.8 copy-start.27
  617.1 2.8 copy-start.27
  629.7 2.8 copy-start.27
  664.8 125.4 %reduce-scatter.20.cloned.1.call-start = ((), (), s32[]{:S(2)}) async-start(), calls=%async_computation.18 | async-start | bytes 4718592 | tf_op jit(solution)/shard_map/reduce_scatter | solution.py:325
  670.1 175.2 %reduce-scatter.18.cloned.1.call-start = ((), (), s32[]{:S(2)}) async-start(), calls=%async_computation.17 | async-start | bytes 4718592 | tf_op jit(solution)/shard_map/reduce_scatter | solution.py:324
  672.1 4.4 copy-start.3
  676.5 223.5 %reduce-scatter.16.cloned.1.call-start = ((), (), s32[]{:S(2)}) async-start(), calls=%async_computation.16 | async-start | bytes 4718592 | tf_op jit(solution)/shard_map/reduce_scatter | solution.py:323
  677.4 4.3 copy-start.15
  681.5 309.2 %reduce-scatter.24.cloned.1.call-start = ((), (), s32[]{:S(2)}) async-start(), calls=%async_computation.20 | async-start | bytes 12976128 | tf_op jit(solution)/shard_map/reduce_scatter | solution.py:328
  689.1 392.1 %reduce-scatter.22.cloned.1.call-start = ((), (), s32[]{:S(2)}) async-start(), calls=%async_computation.19 | async-start | bytes 12976128 | tf_op jit(solution)/shard_map/reduce_scatter | solution.py:327
  696.7 475.2 %reduce-scatter.26.cloned.1.call-start = ((), (), s32[]{:S(2)}) async-start(), calls=%async_computation.21 | async-start | bytes 12976128 | tf_op jit(solution)/shard_map/reduce_scatter | solution.py:329
  705.2 30.5 %copy-start.5 = (bf16[256,1024]{1,0:T(8,128)(2,1)S(1)}, bf16[256,1024]{1,0:T(8,128)(2,1)}, u32[]{:S(2)}) copy-start(bf16[256,1024]{1,0:T(8,128)(2,1)} %param.34) | copy-start | bytes 1572868
  705.2 521.7 %reduce-scatter.14.cloned.1.call-start = ((), (), s32[]{:S(2)}) async-start(), calls=%async_computation.15 | async-start | bytes 4718592 | tf_op jit(solution)/shard_map/reduce_scatter | solution.py:322
  739.7 487.2 %copy-start.40 = (u32[32]{0:T(128)S(1)}, u32[32]{0:T(128)}, u32[]{:S(2)}) copy-start(u32[32]{0:T(128)} %constant.261) | copy-start | bytes 388
  739.7 719.5 %all-reduce.13.cloned.1.call-start = ((), (), s32[]{:S(2)}) async-start(), calls=%async_computation.22 | async-start | bytes 12845056 | tf_op jit(solution)/shard_map/psum | solution.py:342
  1228.2 5.9 copy-start.17
  1228.2 5.9 copy-start.18
  1234.1 3.1 copy-start.11
  1236.4 2.7 copy-start.38
  1459.2 7.8 copy-start.26
  1459.2 8.9 copy-start.25
  1461.3 8.0 copy-start.24
  (28 other events, 52.7 us)
Sparse Core Ops, SparseCore 0:
  12.2 39.5 all-gather.1
  113.1 52.4 all-reduce.8
  271.9 70.6 reduce-scatter.9
  474.5 51.5 all-reduce.10
  664.9 70.6 reduce-scatter.11
  738.9 51.3 reduce-scatter.19
  793.9 51.3 reduce-scatter.17
  848.7 51.2 reduce-scatter.15
  903.9 86.7 reduce-scatter.23
  994.5 86.7 reduce-scatter.21
  1085.1 86.7 reduce-scatter.25
  1175.5 51.3 reduce-scatter.13
  1229.8 229.3 all-reduce.12
